TPU v7x, 512 devices: a whole 4x8x8 slice. The times are simulated.
512 devices in a mesh: rep: 16 (over z, x_hi), exp: 32 (over y, x_lo, core).
Axes of the slice: x: 4 (x_hi: 2, x_lo: 2; x = x_hi * 2 + x_lo), y: 8, z: 8, core: 2. Of those that a mesh axis runs over, the one named last changes fastest.
Arguments:
- activations: bfloat16 [65536, 4096], P(('rep', 'exp')), may hold values from -6 to 6
- grad_hidden: bfloat16 [65536, 1024], P(('rep', 'exp')), may hold values from -6 to 6
- pre_gate: bfloat16 [65536, 1024], P(('rep', 'exp')), may hold values from -12 to 12
- pre_up: bfloat16 [65536, 1024], P(('rep', 'exp')), may hold values from -6 to 6
- modality: int32 [65536], P(('rep', 'exp')), may hold values from 0 to 1, as said below
- expert_index: int32 [65536], P(('rep', 'exp')), may hold values from 0 to 1
- master: float32 [16384, 2048], P(('exp', 'rep')), may hold values from -0.09375 to 0.09375
- first_moment: float32 [16384, 2048], P(('exp', 'rep')), may hold values from -18 to 18
- second_moment: float32 [16384, 2048], P(('exp', 'rep')), may hold values from 200 to 2000
Outputs:
- input_grad: bfloat16 [65536, 4096], P(('rep', 'exp'))
- new_master: float32 [16384, 2048], P(('exp', 'rep'))
- new_first: float32 [16384, 2048], P(('exp', 'rep'))
- new_second: float32 [16384, 2048], P(('exp', 'rep'))
Inputs may be any that keep to these rules, and one draw needn't show every extreme that they name: Among the 128 tokens of one device no expert 2 * modality + expert_index is named more than 48 times; in every replica group of 4096 tokens one expert is named exactly 48 times on every device.
All inputs are finite; a program needn't handle non-finite values.
Results may differ from a plain program's by a relative error of at most 0.019.
Values may be sent and summed in bfloat16 or wider, within the bound.
No kernel may reach another device: no remote copies, remote signals or barrier semaphores. Data moves between devices by JAX's collectives and lax.ppermute only.
A program may use at most 128 MiB of HBM per device.

v0:
```python
import jax
import jax.numpy as jnp
from jax import lax
from jax.sharding import PartitionSpec as P

EXPERTS = 4
CAP = 48
beta_one = 0.9
beta_two = 0.999
learn_rate = 0.02
adam_eps = 1e-08
adam_count = 1000


def from_partner(block, axis, stride):
    count = lax.axis_size(axis)
    route = []
    for low in range(count):
        high = low | 1 << stride
        if high != low and high < count:
            route += [(low, high), (high, low)]
    return lax.ppermute(block, axis, route)


def hidden_grads(saved_rows):
    grad_val = saved_rows[:, 0].astype(jnp.float32)
    gate_val = saved_rows[:, 1].astype(jnp.float32)
    up_val = saved_rows[:, 2].astype(jnp.float32)
    sig = 1.0 / (1.0 + jnp.exp(-gate_val))
    grad_gate = (grad_val * up_val * sig * (1.0 + gate_val * (1.0 - sig))).astype(jnp.bfloat16)
    grad_up = (grad_val * gate_val * sig).astype(jnp.bfloat16)
    return jnp.stack([grad_gate, grad_up], axis=1)


def body(
    activations,
    grad_hidden,
    pre_gate,
    pre_up,
    modality,
    expert_index,
    master,
    first_moment,
    second_moment,
):
    tok_count = activations.shape[0]
    width = activations.shape[1]
    hidden = grad_hidden.shape[1]
    exp_size = lax.axis_size("exp")
    group = exp_size // EXPERTS
    piece_width = width // group
    piece_hidden = hidden // group
    capacity = CAP
    rows_total = exp_size * capacity
    expert = 2 * modality + expert_index
    onehot = (expert[:, None] == jnp.arange(EXPERTS, dtype=jnp.int32)[None, :]).astype(jnp.int32)
    before = jnp.cumsum(onehot, axis=0) - onehot
    slot_pos = jnp.sum(before * onehot, axis=1)
    same_expert = expert[None, None, :] == jnp.arange(EXPERTS, dtype=jnp.int32)[:, None, None]
    same_slot = slot_pos[None, None, :] == jnp.arange(capacity, dtype=jnp.int32)[None, :, None]
    routing = (same_expert & same_slot).astype(jnp.bfloat16)
    x_split = activations.reshape(tok_count, group, piece_width)
    x_send = jnp.einsum("ect,tgd->egcd", routing, x_split, preferred_element_type=jnp.float32)
    x_send = x_send.astype(jnp.bfloat16).reshape(EXPERTS * group, capacity, piece_width)
    saved = jnp.stack([grad_hidden, pre_gate, pre_up], axis=1)
    split_saved = saved.reshape(tok_count, 3, group, piece_hidden)
    parts = jnp.einsum("ect,tsgh->egcsh", routing, split_saved, preferred_element_type=jnp.float32)
    parts = parts.astype(jnp.bfloat16).reshape(EXPERTS * group, capacity, 3 * piece_hidden)
    x_recv, h_recv = (
        lax.all_to_all(x_send, "exp", split_axis=0, concat_axis=0, tiled=True),
        lax.all_to_all(parts, "exp", split_axis=0, concat_axis=0, tiled=True),
    )
    local = hidden_grads(h_recv.reshape(rows_total, 3, piece_hidden))
    blocks = local[None]
    position = lax.axis_index("exp")
    for level in range(group.bit_length() - 1):
        partner = from_partner(blocks, "exp", level)
        upper = position // 2**level % 2 == 1
        blocks = jnp.where(
            upper,
            jnp.concatenate([partner, blocks], axis=0),
            jnp.concatenate([blocks, partner], axis=0),
        )
    grads_flat = jnp.transpose(blocks, (1, 2, 0, 3)).reshape(rows_total, 2 * hidden)
    x_rows = x_recv.reshape(rows_total, piece_width)
    shard_bf = master.astype(jnp.bfloat16)
    dx_rows = lax.dot_general(
        grads_flat,
        lax.all_gather(shard_bf, "rep", axis=0, tiled=True),
        (((1,), (1,)), ((), ())),
        preferred_element_type=jnp.float32,
    )
    dx_send = dx_rows.astype(jnp.bfloat16).reshape(exp_size, capacity, piece_width)
    back = lax.all_to_all(dx_send, "exp", split_axis=0, concat_axis=0, tiled=True)
    back = back.reshape(EXPERTS, group, capacity, piece_width)
    input_grad = jnp.einsum("ect,egcd->tgd", routing, back, preferred_element_type=jnp.float32)
    input_grad = input_grad.reshape(tok_count, width).astype(jnp.bfloat16)
    weight_grad = lax.psum_scatter(
        lax.dot_general(
            x_rows, grads_flat, (((0,), (0,)), ((), ())), preferred_element_type=jnp.float32
        ).astype(jnp.bfloat16),
        "rep",
        scatter_dimension=0,
        tiled=True,
    ).astype(jnp.float32)
    new_first = beta_one * first_moment + (1.0 - beta_one) * weight_grad
    new_second = beta_two * second_moment + (1.0 - beta_two) * weight_grad * weight_grad
    corr_one = 1.0 - beta_one**adam_count
    corr_two = 1.0 - beta_two**adam_count
    update = new_first / corr_one / (jnp.sqrt(new_second / corr_two) + adam_eps)
    new_master = master - learn_rate * update
    return (input_grad, new_master, new_first, new_second)


def solution(mesh):
    in_specs = (
        P(("rep", "exp"), None),
        P(("rep", "exp"), None),
        P(("rep", "exp"), None),
        P(("rep", "exp"), None),
        P(("rep", "exp")),
        P(("rep", "exp")),
        P(("exp", "rep"), None),
        P(("exp", "rep"), None),
        P(("exp", "rep"), None),
    )
    out_specs = (
        P(("rep", "exp"), None),
        P(("exp", "rep"), None),
        P(("exp", "rep"), None),
        P(("exp", "rep"), None),
    )
    return jax.shard_map(body, mesh=mesh, in_specs=in_specs, out_specs=out_specs, check_vma=False)
```

profile of v0, /device:TPU:1, one launch (start us, length us, event | category | flops | bytes accessed | tf_op | source)
XLA Modules:
  0.0 593.7 jit_solution(8257956728713181121)
XLA Ops:
  7.2 0.0 copy-start.5
  7.2 0.7 multiply_add_fusion
  7.9 0.1 fusion.20
  8.0 0.2 reduce_window_sum.11
  8.2 0.2 select_reduce_fusion
  8.4 1.1 copy.25
  9.5 0.2 copy.28
  9.7 1.1 copy.26
  10.8 0.2 copy.29
  11.0 0.0 copy-done.5
  11.0 0.2 copy.27
  11.2 0.2 copy.30
  11.4 0.5 fusion.2
  11.8 1.0 copy.31
  12.9 1.1 reshape.88
  13.9 41.6 %all_to_all.15 = bf16[32,48,384]{2,1,0:T(8,128)(2,1)} all-to-all(bf16[32,48,384]{2,1,0:T(8,128)(2,1)S(1)} %reshape.88), channel_id=1, replica_groups=mesh['rep'=16,'exp'=32] {'exp'}, dimensions={0} | all-to-all | bytes 2359296 | tf_op jit(solution)/shard_map/all_to_all | solution.py:71
  55.5 3.3 reshape.89
  58.8 1.7 fusion.30
  60.5 0.4 fusion.6
  61.0 0.1 maximum_bitcast_fusion.2
  61.1 2.9 collective-permute-start
  64.0 1.9 collective-permute-done
  65.9 0.3 maximum_select_fusion.2
  66.1 0.0 copy-start
  66.2 3.1 collective-permute-start.1
  69.3 0.0 copy-start.1
  69.3 34.4 %collective-permute-done.1 = bf16[2,1536,2,128]{3,1,2,0:T(8,128)(2,1)} collective-permute-done((bf16[2,1536,2,128]{3,1,2,0:T(8,128)(2,1)S(1)}, bf16[2,1536,2,128]{3,1,2,0:T(8,128)(2,1)}, u32[]{:S(2)}, u32[]{:S(2)}) %collective-permute-start.1) | collective-permute-done | bytes 1572896 | tf_op jit(solution)/shard_map/ppermute | solution.py:22
  103.8 3.1 maximum_select_fusion.1
  106.8 2.8 collective-permute-start.2
  109.6 1.7 convolution_convert_fusion.2
  111.3 5.8 all-to-all-start.2
  117.1 0.0 reduce-scatter.2.cloned.1.call-start
  117.2 68.5 %collective-permute-done.2 = bf16[4,1536,2,128]{3,1,2,0:T(8,128)(2,1)} collective-permute-done((bf16[4,1536,2,128]{3,1,2,0:T(8,128)(2,1)S(1)}, bf16[4,1536,2,128]{3,1,2,0:T(8,128)(2,1)}, u32[]{:S(2)}, u32[]{:S(2)}) %collective-permute-start.2) | collective-permute-done | bytes 3145760 | tf_op jit(solution)/shard_map/ppermute | solution.py:22
  185.7 6.6 %fusion = bf16[1536,2,8,128]{3,0,1,2:T(8,128)(2,1)} fusion(bf16[4,1536,2,128]{3,1,2,0:T(8,128)(2,1)S(1)} %maximum_select_fusion.1, bf16[4,1536,2,128]{3,1,2,0:T(8,128)(2,1)} %collective-permute-done.2, pred[]{:T(512)S(6)} %eq.71), kind=kLoop, calls=%fused_computation.1 | loop fusion | flops 9437184 | bytes 12582913 | tf_op jit(solution)/shard_map/transpose | solution.py:84
  192.3 8.6 %copy.35 = bf16[1536,2,8,128]{0,3,2,1:T(8,128)(2,1)} copy(bf16[1536,2,8,128]{3,0,1,2:T(8,128)(2,1)} %fusion) | data formatting | bytes 12582912 | tf_op jit(solution)/shard_map/transpose | solution.py:84
  200.9 11.8 %all-to-all-done.2 = bf16[32,48,512]{2,1,0:T(8,128)(2,1)} async-done(((bf16[32,48,512]{2,1,0:T(8,128)(2,1)}), bf16[32,48,512]{2,1,0:T(8,128)(2,1)}, u32[]{:S(2)}, u32[]{:S(2)}) %all-to-all-start.2) | async-done | bytes 1572896 | tf_op jit(solution)/shard_map/all_to_all | solution.py:70
  212.7 8.1 %convolution_convert_fusion = bf16[512,2048]{1,0:T(8,128)(2,1)} fusion(bf16[1536,512]{1,0:T(8,128)(2,1)} %bitcast.20, bf16[1536,2048]{0,1:T(8,128)(2,1)} %bitcast.54), kind=kOutput, calls=%fused_computation.5 | convolution fusion | flops 3222274048 | bytes 9961472 | tf_op jit(solution)/shard_map/dot_general | solution.py:99
  220.8 0.0 reduce-scatter.2.cloned.1.call-update
  220.8 0.2 all-gather.2.cloned.1.call-start
  221.1 210.8 %reduce-scatter.2.cloned.1.call-done = bf16[32,2048]{1,0:T(8,128)(2,1)} async-done(((bf16[512,2048]{1,0:T(8,128)(2,1)}), bf16[32,2048]{1,0:T(8,128)(2,1)}) %reduce-scatter.2.cloned.1.call-update) | async-done | bytes 131088 | tf_op jit(solution)/shard_map/reduce_scatter | solution.py:98
  431.9 1.9 multiply_subtract_fusion
  433.8 0.0 all-gather.2.cloned.1.call-update
  433.9 92.5 %all-gather.2.cloned.1.call-done = bf16[512,2048]{1,0:T(8,128)(2,1)} async-done(((bf16[32,2048]{1,0:T(8,128)(2,1)}), bf16[512,2048]{1,0:T(8,128)(2,1)}) %all-gather.2.cloned.1.call-update) | async-done | bytes 2097168 | tf_op jit(solution)/shard_map/all_gather | solution.py:89
  526.3 6.9 %convolution_convert_fusion.1 = bf16[1536,512]{1,0:T(8,128)(2,1)S(1)} fusion(bf16[1536,2048]{0,1:T(8,128)(2,1)} %bitcast.55, bf16[512,2048]{1,0:T(8,128)(2,1)} %all-gather.2.cloned.1.call-done), kind=kOutput, calls=%fused_computation.6 | convolution fusion | flops 3222011904 | bytes 9961472 | tf_op jit(solution)/shard_map/dot_general | solution.py:87
  533.2 50.5 %all_to_all.16 = bf16[32,48,512]{2,1,0:T(8,128)(2,1)S(1)} all-to-all(bf16[32,48,512]{2,1,0:T(8,128)(2,1)S(1)} %bitcast.59), channel_id=1, replica_groups=mesh['rep'=16,'exp'=32] {'exp'}, dimensions={0} | all-to-all | bytes 3145728 | tf_op jit(solution)/shard_map/all_to_all | solution.py:94
  583.8 0.9 copy.55
  584.6 0.8 dot_general.22
  585.4 1.5 fusion.1
  (10 shorter events, 0.0 us)
Async XLA Ops:
  7.2 3.8 copy-start.5
  61.1 4.8 collective-permute-start
  66.1 3.2 copy-start
  66.2 37.6 %collective-permute-start.1 = (bf16[2,1536,2,128]{3,1,2,0:T(8,128)(2,1)S(1)}, bf16[2,1536,2,128]{3,1,2,0:T(8,128)(2,1)}, u32[]{:S(2)}, u32[]{:S(2)}) collective-permute-start(bf16[2,1536,2,128]{3,1,2,0:T(8,128)(2,1)S(1)} %maximum_select_fusion.2), channel_id=1, source_target_pairs={{0,2},{2,0},{1,3},{3,1},{4,6},{6,4},{5,7},{7,5},{8,10},{10,8},{9,1... | collective-permute-start | bytes 4718600 | tf_op jit(solution)/shard_map/ppermute | solution.py:22
  69.3 40.3 %copy-start.1 = (bf16[128,4096]{1,0:T(8,128)(2,1)S(1)}, bf16[128,4096]{1,0:T(8,128)(2,1)}, u32[]{:S(2)}) copy-start(bf16[128,4096]{1,0:T(8,128)(2,1)} %param.9) | copy-start | bytes 3145732
  106.8 78.8 %collective-permute-start.2 = (bf16[4,1536,2,128]{3,1,2,0:T(8,128)(2,1)S(1)}, bf16[4,1536,2,128]{3,1,2,0:T(8,128)(2,1)}, u32[]{:S(2)}, u32[]{:S(2)}) collective-permute-start(bf16[4,1536,2,128]{3,1,2,0:T(8,128)(2,1)S(1)} %maximum_select_fusion.1), channel_id=1, source_target_pairs={{0,4},{4,0},{1,5},{5,1},{2,6},{6,2},{3,7},{7,3},{8,12},{12,8},{9,1... | collective-permute-start | bytes 9437192 | tf_op jit(solution)/shard_map/ppermute | solution.py:22
  111.3 101.4 %all-to-all-start.2 = ((bf16[32,48,512]{2,1,0:T(8,128)(2,1)}), bf16[32,48,512]{2,1,0:T(8,128)(2,1)}, u32[]{:S(2)}, u32[]{:S(2)}) async-start(bf16[32,48,512]{2,1,0:T(8,128)(2,1)} %bitcast.56), calls=%async_computation.2 | async-start | bytes 3145728 | tf_op jit(solution)/shard_map/all_to_all | solution.py:70
  117.1 314.8 %reduce-scatter.2.cloned.1.call-start = ((), (), s32[]{:S(2)}) async-start(), calls=%async_computation.5 | async-start | bytes 2228224 | tf_op jit(solution)/shard_map/reduce_scatter | solution.py:98
  220.8 211.1 %copy-start.2 = (f32[32,2048]{1,0:T(8,128)S(1)}, f32[32,2048]{1,0:T(8,128)}, u32[]{:S(2)}) copy-start(f32[32,2048]{1,0:T(8,128)} %param.15) | copy-start | bytes 786436
  220.8 211.1 %copy-start.3 = (f32[32,2048]{1,0:T(8,128)S(1)}, f32[32,2048]{1,0:T(8,128)}, u32[]{:S(2)}) copy-start(f32[32,2048]{1,0:T(8,128)} %param.17) | copy-start | bytes 786436
  220.8 211.1 %copy-start.4 = (f32[32,2048]{1,0:T(8,128)S(1)}, f32[32,2048]{1,0:T(8,128)}, u32[]{:S(2)}) copy-start(f32[32,2048]{1,0:T(8,128)} %param.16) | copy-start | bytes 786436
  220.8 305.5 %all-gather.2.cloned.1.call-start = ((), (), s32[]{:S(2)}) async-start(), calls=%async_computation.4 | async-start | bytes 2228224 | tf_op jit(solution)/shard_map/all_gather | solution.py:89
Sparse Core Ops, SparseCore 0:
  221.0 210.9 reduce-scatter.1
  435.6 90.6 all-gather.1
where the time goes:
time: 595 us; the launch traced here: 594 us
  waiting for transfers between devices  420 us (71%)
  blocking collectives  92.1 us (15%)
  local copies, waits for them, and re-layouts  20.4 us (3%)
  matrix products  18.6 us (3%)
  starting transfers between devices  14.8 us (2%)
  between operations  14.3 us (2%)
  other arithmetic  13.6 us (2%)
    reduce_scatter x1, waiting for transfers between devices, body(): lax.psum_scatter(lax.dot_general(x_rows, grads_flat, (((0,), (0,)), ((),...  211 us
    ppermute x3, waiting for transfers between devices, from_partner(): return lax.ppermute(block, axis, route)  105 us
    all_gather x1, waiting for transfers between devices, body(): lax.all_gather(shard_bf, 'rep', axis=0, tiled=True)  92.5 us
    all_to_all x1, blocking collectives, body(): lax.all_to_all(dx_send, 'exp', split_axis=0, concat_axis=0, tiled=True)  50.5 us
    all_to_all x1, blocking collectives, body(): lax.all_to_all(parts, 'exp', split_axis=0, concat_axis=0, tiled=True)  41.6 us
  transfers between devices with their start and end apart: 6, of which 6 were waited for; matrix products, arithmetic and copies ran while one was open for 3% of the time, Pallas kernels for 0%

commit v1 on v0

--- a/solution.py
+++ b/solution.py
@@ -86,7 +86,9 @@
     shard_bf = master.astype(jnp.bfloat16)
     dx_rows = lax.dot_general(
         grads_flat,
-        lax.all_gather(shard_bf, "rep", axis=0, tiled=True),
+        jnp.concatenate(
+            lax.all_to_all(jnp.stack([shard_bf] * lax.axis_size("rep")), "rep", 0, 0), axis=0
+        ),
         (((1,), (1,)), ((), ())),
         preferred_element_type=jnp.float32,
     )

time: 595 us -> 554 us (0.931)
  waiting for transfers between devices: 420 us -> 327 us
  blocking collectives: 92.1 us -> 148 us
    all_gather x1 -> x0, waiting for transfers between devices: 92.5 us -> none  [body(): lax.all_gather(shard_bf, 'rep', axis=0, tiled=True)]
    all_to_all x0 -> x1, blocking collectives: none -> 51.1 us  [body(): lax.all_to_all(jnp.stack([shard_bf] * lax.axis_size('rep')), 'rep', 0, 0)]
  transfers between devices with their start and end apart: 6 -> 5, of which waited for: 6 -> 5; matrix products, arithmetic and copies ran while one was open for 3% -> 3% of each run, Pallas kernels for 0% -> 0%
where the time goes in v1:
time: 554 us
  waiting for transfers between devices  327 us (59%)
  blocking collectives  148 us (27%)
  local copies, waits for them, and re-layouts  20.6 us (4%)
  matrix products  15.2 us (3%)
  starting transfers between devices  14.8 us (3%)
  between operations  14.3 us (3%)
  other arithmetic  13.6 us (2%)
    reduce_scatter x1, waiting for transfers between devices, body(): lax.psum_scatter(lax.dot_general(x_rows, grads_flat, (((0,), (0,)), ((),...  211 us
    ppermute x3, waiting for transfers between devices, from_partner(): return lax.ppermute(block, axis, route)  105 us
    all_to_all x1, blocking collectives, body(): lax.all_to_all(dx_send, 'exp', split_axis=0, concat_axis=0, tiled=True)  54.9 us
    all_to_all x1, blocking collectives, body(): lax.all_to_all(jnp.stack([shard_bf] * lax.axis_size('rep')), 'rep', 0, 0)  51.1 us
    all_to_all x1, blocking collectives, body(): lax.all_to_all(parts, 'exp', split_axis=0, concat_axis=0, tiled=True)  41.6 us
    all_to_all x1, waiting for transfers between devices, body(): lax.all_to_all(x_send, 'exp', split_axis=0, concat_axis=0, tiled=True)  11.7 us
  transfers between devices with their start and end apart: 5, of which 5 were waited for; matrix products, arithmetic and copies ran while one was open for 3% of the time, Pallas kernels for 0%

profile of v1, /device:TPU:1, one launch (start us, length us, event | category | flops | bytes accessed | tf_op | source)
XLA Modules:
  0.0 553.5 jit_solution(2445574595005367190)
XLA Ops:
  7.2 0.0 copy-start.6
  7.2 0.7 multiply_add_fusion
  7.9 0.1 fusion.20
  8.0 0.2 reduce_window_sum.11
  8.2 0.2 select_reduce_fusion
  8.4 1.1 copy.25
  9.5 0.2 copy.28
  9.7 1.1 copy.26
  10.8 0.2 copy.29
  11.0 0.0 copy-done.6
  11.0 0.2 copy.27
  11.2 0.2 copy.30
  11.4 0.5 fusion.2
  11.8 1.0 copy.31
  12.9 1.1 reshape.93
  13.9 41.6 %all_to_all.20 = bf16[32,48,384]{2,1,0:T(8,128)(2,1)} all-to-all(bf16[32,48,384]{2,1,0:T(8,128)(2,1)S(1)} %reshape.93), channel_id=1, replica_groups=mesh['rep'=16,'exp'=32] {'exp'}, dimensions={0} | all-to-all | bytes 2359296 | tf_op jit(solution)/shard_map/all_to_all | solution.py:71
  55.5 3.3 reshape.94
  58.8 1.7 fusion.30
  60.5 0.4 fusion.6
  61.0 0.1 maximum_bitcast_fusion.2
  61.1 2.9 collective-permute-start
  64.0 1.9 collective-permute-done
  65.9 0.3 maximum_select_fusion.2
  66.2 0.0 copy-start.1
  66.2 3.1 collective-permute-start.1
  69.3 0.0 copy-done.1
  69.3 0.0 copy-start.2
  69.3 34.4 %collective-permute-done.1 = bf16[2,1536,2,128]{3,1,2,0:T(8,128)(2,1)} collective-permute-done((bf16[2,1536,2,128]{3,1,2,0:T(8,128)(2,1)S(1)}, bf16[2,1536,2,128]{3,1,2,0:T(8,128)(2,1)}, u32[]{:S(2)}, u32[]{:S(2)}) %collective-permute-start.1) | collective-permute-done | bytes 1572896 | tf_op jit(solution)/shard_map/ppermute | solution.py:22
  103.8 3.1 maximum_select_fusion.1
  106.9 2.8 collective-permute-start.2
  109.6 1.7 convolution_convert_fusion.2
  111.4 5.8 %all-to-all-start.3 = ((bf16[32,48,512]{2,1,0:T(8,128)(2,1)}), bf16[32,48,512]{2,1,0:T(8,128)(2,1)}, u32[]{:S(2)}, u32[]{:S(2)}) async-start(bf16[32,48,512]{2,1,0:T(8,128)(2,1)} %bitcast.57), calls=%async_computation.3 | async-start | bytes 3145728 | tf_op jit(solution)/shard_map/all_to_all | solution.py:70
  117.1 0.2 reduce-scatter.2.cloned.1.call-start
  117.4 68.3 %collective-permute-done.2 = bf16[4,1536,2,128]{3,1,2,0:T(8,128)(2,1)} collective-permute-done((bf16[4,1536,2,128]{3,1,2,0:T(8,128)(2,1)S(1)}, bf16[4,1536,2,128]{3,1,2,0:T(8,128)(2,1)}, u32[]{:S(2)}, u32[]{:S(2)}) %collective-permute-start.2) | collective-permute-done | bytes 3145760 | tf_op jit(solution)/shard_map/ppermute | solution.py:22
  185.7 6.7 %fusion = bf16[1536,2,8,128]{3,0,1,2:T(8,128)(2,1)} fusion(bf16[4,1536,2,128]{3,1,2,0:T(8,128)(2,1)S(1)} %maximum_select_fusion.1, bf16[4,1536,2,128]{3,1,2,0:T(8,128)(2,1)} %collective-permute-done.2, pred[]{:T(512)S(6)} %eq.71), kind=kLoop, calls=%fused_computation.1 | loop fusion | flops 9437184 | bytes 12582913 | tf_op jit(solution)/shard_map/transpose | solution.py:84
  192.4 8.6 %copy.35 = bf16[1536,2,8,128]{0,3,2,1:T(8,128)(2,1)} copy(bf16[1536,2,8,128]{3,0,1,2:T(8,128)(2,1)} %fusion) | data formatting | bytes 12582912 | tf_op jit(solution)/shard_map/transpose | solution.py:84
  201.0 11.7 %all-to-all-done.3 = bf16[32,48,512]{2,1,0:T(8,128)(2,1)} async-done(((bf16[32,48,512]{2,1,0:T(8,128)(2,1)}), bf16[32,48,512]{2,1,0:T(8,128)(2,1)}, u32[]{:S(2)}, u32[]{:S(2)}) %all-to-all-start.3) | async-done | bytes 1572896 | tf_op jit(solution)/shard_map/all_to_all | solution.py:70
  212.7 8.1 %convolution_convert_fusion = bf16[512,2048]{1,0:T(8,128)(2,1)} fusion(bf16[1536,512]{1,0:T(8,128)(2,1)} %bitcast.21, bf16[1536,2048]{0,1:T(8,128)(2,1)} %bitcast.55), kind=kOutput, calls=%fused_computation.5 | convolution fusion | flops 3222274048 | bytes 9961472 | tf_op jit(solution)/shard_map/dot_general | solution.py:101
  220.8 0.0 reduce-scatter.2.cloned.1.call-update
  220.9 211.0 %reduce-scatter.2.cloned.1.call-done = bf16[32,2048]{1,0:T(8,128)(2,1)} async-done(((bf16[512,2048]{1,0:T(8,128)(2,1)}), bf16[32,2048]{1,0:T(8,128)(2,1)}) %reduce-scatter.2.cloned.1.call-update) | async-done | bytes 131088 | tf_op jit(solution)/shard_map/reduce_scatter | solution.py:100
  431.9 1.9 multiply_subtract_fusion
  433.8 0.2 stack.17
  434.0 51.1 %all_to_all.21 = bf16[16,32,2048]{2,1,0:T(8,128)(2,1)S(1)} all-to-all(bf16[16,32,2048]{2,1,0:T(8,128)(2,1)S(1)} %stack.17), channel_id=1, replica_groups=mesh['rep'=16,'exp'=32] {'rep'}, dimensions={0} | all-to-all | bytes 4194304 | tf_op jit(solution)/shard_map/all_to_all | solution.py:90
  485.2 3.5 convolution_convert_fusion.1
  488.6 54.9 %all_to_all.22 = bf16[32,48,512]{2,1,0:T(8,128)(2,1)S(1)} all-to-all(bf16[32,48,512]{2,1,0:T(8,128)(2,1)S(1)} %bitcast.61), channel_id=1, replica_groups=mesh['rep'=16,'exp'=32] {'exp'}, dimensions={0} | all-to-all | bytes 3145728 | tf_op jit(solution)/shard_map/all_to_all | solution.py:96
  543.6 0.9 copy.55
  544.4 0.8 dot_general.22
  545.2 1.5 fusion.1
  (11 shorter events, 0.0 us)
Async XLA Ops:
  7.2 3.8 copy-start.6
  61.1 4.8 collective-permute-start
  66.2 3.2 copy-start.1
  66.2 37.6 %collective-permute-start.1 = (bf16[2,1536,2,128]{3,1,2,0:T(8,128)(2,1)S(1)}, bf16[2,1536,2,128]{3,1,2,0:T(8,128)(2,1)}, u32[]{:S(2)}, u32[]{:S(2)}) collective-permute-start(bf16[2,1536,2,128]{3,1,2,0:T(8,128)(2,1)S(1)} %maximum_select_fusion.2), channel_id=1, source_target_pairs={{0,2},{2,0},{1,3},{3,1},{4,6},{6,4},{5,7},{7,5},{8,10},{10,8},{9,1... | collective-permute-start | bytes 4718600 | tf_op jit(solution)/shard_map/ppermute | solution.py:22
  69.3 40.3 %copy-start.2 = (bf16[128,4096]{1,0:T(8,128)(2,1)S(1)}, bf16[128,4096]{1,0:T(8,128)(2,1)}, u32[]{:S(2)}) copy-start(bf16[128,4096]{1,0:T(8,128)(2,1)} %param.9) | copy-start | bytes 3145732
  106.9 78.8 %collective-permute-start.2 = (bf16[4,1536,2,128]{3,1,2,0:T(8,128)(2,1)S(1)}, bf16[4,1536,2,128]{3,1,2,0:T(8,128)(2,1)}, u32[]{:S(2)}, u32[]{:S(2)}) collective-permute-start(bf16[4,1536,2,128]{3,1,2,0:T(8,128)(2,1)S(1)} %maximum_select_fusion.1), channel_id=1, source_target_pairs={{0,4},{4,0},{1,5},{5,1},{2,6},{6,2},{3,7},{7,3},{8,12},{12,8},{9,1... | collective-permute-start | bytes 9437192 | tf_op jit(solution)/shard_map/ppermute | solution.py:22
  111.4 101.4 %all-to-all-start.3 = ((bf16[32,48,512]{2,1,0:T(8,128)(2,1)}), bf16[32,48,512]{2,1,0:T(8,128)(2,1)}, u32[]{:S(2)}, u32[]{:S(2)}) async-start(bf16[32,48,512]{2,1,0:T(8,128)(2,1)} %bitcast.57), calls=%async_computation.3 | async-start | bytes 3145728 | tf_op jit(solution)/shard_map/all_to_all | solution.py:70
  117.1 314.7 %reduce-scatter.2.cloned.1.call-start = ((), (), s32[]{:S(2)}) async-start(), calls=%async_computation.5 | async-start | bytes 2228224 | tf_op jit(solution)/shard_map/reduce_scatter | solution.py:100
  220.8 211.0 %copy-start.3 = (f32[32,2048]{1,0:T(8,128)S(1)}, f32[32,2048]{1,0:T(8,128)}, u32[]{:S(2)}) copy-start(f32[32,2048]{1,0:T(8,128)} %param.15) | copy-start | bytes 786436
  220.8 211.0 %copy-start.4 = (f32[32,2048]{1,0:T(8,128)S(1)}, f32[32,2048]{1,0:T(8,128)}, u32[]{:S(2)}) copy-start(f32[32,2048]{1,0:T(8,128)} %param.17) | copy-start | bytes 786436
  220.8 211.0 %copy-start.5 = (f32[32,2048]{1,0:T(8,128)S(1)}, f32[32,2048]{1,0:T(8,128)}, u32[]{:S(2)}) copy-start(f32[32,2048]{1,0:T(8,128)} %param.16) | copy-start | bytes 786436
  433.8 51.4 %copy-start = (bf16[1536,2,8,128]{0,3,2,1:T(8,128)(2,1)S(1)}, bf16[1536,2,8,128]{0,3,2,1:T(8,128)(2,1)}, u32[]{:S(2)}) copy-start(bf16[1536,2,8,128]{0,3,2,1:T(8,128)(2,1)} %copy.35) | copy-start | bytes 18874372
Sparse Core Ops, SparseCore 0:
  221.0 210.8 reduce-scatter.1
